TPU v7x, 128 devices: a whole 4x4x4 slice. The times are simulated.
128 devices in a mesh: dp: 8 (over x, y_lo), mp: 16 (over z, y_hi, core).
Axes of the slice: x: 4, y: 4 (y_hi: 2, y_lo: 2; y = y_hi * 2 + y_lo), z: 4, core: 2. Of those that a mesh axis runs over, the one named last changes fastest.
Arguments:
- features: bfloat16 [16384, 16384], P('dp', 'mp'), may hold values from -6 to 6
- weights: bfloat16 [16384, 16384], P('mp', 'dp'), may hold values from -6 to 6
- u_rows: float32 [1024, 16384], P('mp', 'dp'), as said below
- keep_pairs: int32 [2, 128, 2], replicated, may hold values from 0 to 3, as said below
Outputs:
- pruned_weights: bfloat16 [16384, 16384], P('mp', 'dp')
- hessian_rows: float32 [1024, 16384], P('dp', 'mp')
Inputs may be any that keep to these rules, and one draw needn't show every extreme that they name: Row r of u_rows is zero left of column r, and its entry in column r is 1 or more. `keep_pairs`: the two positions of a pair differ and the first is the smaller.
All inputs are finite; a program needn't handle non-finite values.
Results may differ from a plain program's by a relative error of at most 0.012.
Values may be sent and summed in bfloat16 or wider, within the bound.
A program may use at most 128 MiB of HBM per device.

v0:
```python
import jax
import jax.numpy as jnp
from jax import lax
from jax.sharding import PartitionSpec as P

B = 512
PANELS = 2
WIN = 1024


def rows_for(lines, devices):
    spare = -len(lines) % devices
    return jnp.pad(lines, [(0, spare)] + [(0, 0)] * (lines.ndim - 1))


def broadcast_by_parts(x, axis, root):
    lines = jnp.where(lax.axis_index(axis) == root, x, jnp.zeros_like(x)).reshape(
        -1, *x.shape[1:][-1:]
    )
    padded = rows_for(lines, lax.axis_size(axis))
    own = lax.psum_scatter(padded, axis, scatter_dimension=0, tiled=True)
    return lax.all_gather(own, axis, axis=0, tiled=True)[: len(lines)].reshape(x.shape)


def cut_along(x, dim, devices):
    dims = x.shape
    pieces = x.reshape(*dims[:dim], devices, dims[dim] // devices, *dims[dim + 1 :])
    return jnp.moveaxis(pieces, dim, 0)


def summed_on_arrival(x, axis, dim):
    pieces = cut_along(x, dim, lax.axis_size(axis))
    arrived = lax.all_to_all(pieces, axis, split_axis=0, concat_axis=0, tiled=True)
    return arrived.astype(jnp.float32).sum(axis=0)


def keep_columns(pairs):
    positions = jnp.arange(4, dtype=jnp.int32)
    selected = (pairs[:, 0:1] == positions) | (pairs[:, 1:2] == positions)
    return selected.astype(jnp.float32).reshape(-1)


def solve_errors(panel_cols, diag_block, keep):
    pruned = 1.0 - keep
    system = diag_block * pruned[:, None] * pruned[None, :] + jnp.diag(keep)
    width = system.shape[0]
    ident = jnp.eye(width, dtype=jnp.float32)
    diag_vals = jnp.diagonal(system)
    strict = system / diag_vals[:, None] - ident
    inverse = ident - strict
    power = strict
    for level in range((width - 1).bit_length() - 1):
        power = jnp.dot(power, power, precision=lax.Precision.HIGHEST)
        inverse = inverse + jnp.dot(inverse, power, precision=lax.Precision.HIGHEST)
    scaled = jnp.dot(panel_cols * pruned[None, :], inverse, precision=lax.Precision.HIGHEST)
    return scaled / diag_vals[None, :]


def panel_solve(lead_cols, corner, keep_list):
    error_list = []
    for panel in range(PANELS):
        panel_cols = lead_cols[:, panel * B : (panel + 1) * B]
        for earlier in range(panel):
            panel_cols = panel_cols - jnp.dot(
                error_list[earlier],
                corner[earlier * B : (earlier + 1) * B, panel * B : (panel + 1) * B],
                precision=lax.Precision.HIGHEST,
            )
        diag_block = corner[panel * B : (panel + 1) * B, panel * B : (panel + 1) * B]
        error_list.append(solve_errors(panel_cols, diag_block, keep_list[panel]))
    return jnp.concatenate(error_list, axis=1)


def body(features, weights, u_rows, keep_pairs):
    window = broadcast_by_parts(features, "mp", 0)
    hessian_scale = 2.0 / (features.shape[0] * lax.axis_size("dp"))
    hessian_rows = (
        summed_on_arrival(
            lax.dot_general(
                window, features, (((0,), (0,)), ((), ())), preferred_element_type=jnp.float32
            ).astype(jnp.bfloat16),
            "dp",
            0,
        )
        * hessian_scale
    )
    factors = lax.all_gather(u_rows.astype(jnp.bfloat16), "mp", axis=0, tiled=True).astype(
        u_rows.dtype
    )
    current = weights.astype(jnp.float32)
    keep_list = [keep_columns(keep_pairs[panel]) for panel in range(PANELS)]
    is_owner = lax.axis_index("dp") == 0

    def owner_solve():
        return panel_solve(current[:, :WIN], factors[:, :WIN], keep_list)

    def no_solve():
        return jnp.zeros((current.shape[0], WIN), jnp.float32)

    local_errors = lax.cond(is_owner, owner_solve, no_solve)
    errors = broadcast_by_parts(local_errors, "dp", 0)
    updated = current - jnp.dot(errors, factors, precision=lax.Precision.HIGHEST)
    column_mask = jnp.concatenate(keep_list + [jnp.ones((current.shape[1] - WIN,), jnp.float32)])
    column_mask = jnp.where(is_owner, column_mask, 1.0)
    pruned_weights = (updated * column_mask[None, :]).astype(jnp.bfloat16)
    return (pruned_weights, hessian_rows)


def solution(mesh):
    in_specs = (P("dp", "mp"), P("mp", "dp"), P("mp", "dp"), P())
    out_specs = (P("mp", "dp"), P("dp", "mp"))
    return jax.shard_map(body, mesh=mesh, in_specs=in_specs, out_specs=out_specs, check_vma=False)
```

profile of v0, /device:TPU:59, one launch (start us, length us, event | category | flops | bytes accessed | tf_op | source)
XLA Modules:
  0.0 453.0 jit_solution(7278853949540482745)
XLA Ops:
  7.2 0.0 all-gather.4.cloned.1.call-start
  7.2 1.8 convert_element_type.53
  9.0 0.0 all-gather.4.cloned.1.call-update
  9.0 0.0 reduce-scatter.5.cloned.1.call-start
  9.1 2.3 broadcast_select_fusion
  11.3 0.0 reduce-scatter.5.cloned.1.call-update
  11.4 0.0 reduce-scatter.3.cloned.1.call-start
  11.4 0.6 copy-done.1
  12.0 0.1 fusion.20
  12.1 0.1 reshape.65
  12.2 0.1 fusion.22
  12.3 0.1 reshape.66
  12.5 6.5 %convert_element_type.49 = f32[1024,2048]{1,0:T(8,128)} convert(bf16[1024,2048]{1,0:T(8,128)(2,1)} %param.7) | non-fusion elementwise | flops 2097152 | bytes 12582912 | tf_op jit(solution)/shard_map/convert_element_type | solution.py:90
  18.9 46.3 %all-gather.4.cloned.1.call-done = bf16[1024,2048]{1,0:T(8,128)(2,1)} async-done(((bf16[64,2048]{1,0:T(8,128)(2,1)}), bf16[1024,2048]{1,0:T(8,128)(2,1)}) %all-gather.4.cloned.1.call-update) | async-done | bytes 4194320 | tf_op jit(solution)/shard_map/all_gather | solution.py:87
  65.3 6.5 %convert_element_type.54 = f32[1024,2048]{1,0:T(8,128)} convert(bf16[1024,2048]{1,0:T(8,128)(2,1)} %all-gather.4.cloned.1.call-done) | non-fusion elementwise | flops 2097152 | bytes 12582912 | tf_op jit(solution)/shard_map/convert_element_type | solution.py:87
  71.8 2.5 conditional.1
  71.8 2.5 broadcast.43
  74.3 2.8 broadcast_select_fusion.1
  77.2 0.0 reduce-scatter.3.cloned.1.call-update
  77.2 0.0 all-gather.8.cloned.1.call-start
  77.2 69.9 %reduce-scatter.5.cloned.1.call-done = bf16[128,1024]{1,0:T(8,128)(2,1)} async-done(((bf16[2048,1024]{1,0:T(8,128)(2,1)}), bf16[128,1024]{1,0:T(8,128)(2,1)}) %reduce-scatter.5.cloned.1.call-update) | async-done | bytes 262160 | tf_op jit(solution)/shard_map/reduce_scatter | solution.py:21
  147.1 0.0 all-gather.8.cloned.1.call-update
  147.1 0.0 all-gather.6.cloned.1.call-start
  147.2 108.3 %reduce-scatter.3.cloned.1.call-done = f32[128,1024]{0,1:T(8,128)} async-done(((f32[1024,1024]{0,1:T(8,128)}), f32[128,1024]{0,1:T(8,128)}) %reduce-scatter.3.cloned.1.call-update) | async-done | bytes 524304 | tf_op jit(solution)/shard_map/reduce_scatter | solution.py:21
  255.5 56.5 %all-gather.8.cloned.1.call-done = bf16[2048,1024]{1,0:T(8,128)(2,1)} async-done(((bf16[128,1024]{1,0:T(8,128)(2,1)}), bf16[2048,1024]{1,0:T(8,128)(2,1)}) %all-gather.8.cloned.1.call-update) | async-done | bytes 4194320 | tf_op jit(solution)/shard_map/all_gather | solution.py:22
  312.0 9.4 %convolution_convert_fusion = bf16[1024,1024]{1,0:T(8,128)(2,1)} fusion(bf16[2048,1024]{1,0:T(8,128)(2,1)} %all-gather.8.cloned.1.call-done, bf16[2048,1024]{1,0:T(8,128)(2,1)} %param.6), kind=kOutput, calls=%fused_computation.48 | convolution fusion | flops 4296015872 | bytes 10485760 | tf_op jit(solution)/shard_map/dot_general | solution.py:79
  321.3 5.1 %all-to-all-start = ((bf16[8,128,1024]{2,1,0:T(8,128)(2,1)}), bf16[8,128,1024]{2,1,0:T(8,128)(2,1)S(1)}, u32[]{:S(2)}, u32[]{:S(2)}) async-start(bf16[8,128,1024]{2,1,0:T(8,128)(2,1)} %bitcast.81), calls=%async_computation.2 | async-start | bytes 4194304 | tf_op jit(solution)/shard_map/all_to_all | solution.py:33
  326.5 32.2 %all-to-all-done = bf16[8,128,1024]{2,1,0:T(8,128)(2,1)S(1)} async-done(((bf16[8,128,1024]{2,1,0:T(8,128)(2,1)}), bf16[8,128,1024]{2,1,0:T(8,128)(2,1)S(1)}, u32[]{:S(2)}, u32[]{:S(2)}) %all-to-all-start) | async-done | bytes 2097184 | tf_op jit(solution)/shard_map/all_to_all | solution.py:33
  358.7 0.3 convert_reduce_fusion
  359.1 0.8 broadcast_multiply_fusion
  359.9 68.5 %all-gather.6.cloned.1.call-done = f32[1024,1024]{0,1:T(8,128)} async-done(((f32[128,1024]{0,1:T(8,128)}), f32[1024,1024]{0,1:T(8,128)}) %all-gather.6.cloned.1.call-update) | async-done | bytes 4194320 | tf_op jit(solution)/shard_map/all_gather | solution.py:22
  428.4 18.0 %multiply_convert_fusion = bf16[1024,2048]{1,0:T(8,128)(2,1)} fusion(f32[2048]{0:T(1024)S(1)} %maximum_select_fusion, f32[1024,1024]{0,1:T(8,128)} %all-gather.6.cloned.1.call-done, bf16[1024,2048]{1,0:T(8,128)(2,1)} %all-gather.4.cloned.1.call-done, bf16[1024,2048]{1,0:T(8,128)(2,1)} %param.7), kind=kOutput, calls=%fused_computation.44 | convolution fusion | flops 25778192384 | bytes 16785408 | tf_op jit(solution)/shard_map/dot_general | solution.py:102
  (6 shorter events, 0.0 us)
Async XLA Ops:
  7.2 58.1 %all-gather.4.cloned.1.call-start = ((), (), s32[]{:S(2)}) async-start(), calls=%async_computation.3 | async-start | bytes 4456448 | tf_op jit(solution)/shard_map/all_gather | solution.py:87
  9.0 138.1 %reduce-scatter.5.cloned.1.call-start = ((), (), s32[]{:S(2)}) async-start(), calls=%async_computation.6 | async-start | bytes 4456448 | tf_op jit(solution)/shard_map/reduce_scatter | solution.py:21
  11.3 0.7 copy-start.1
  11.4 244.1 %reduce-scatter.3.cloned.1.call-start = ((), (), s32[]{:S(2)}) async-start(), calls=%async_computation.4 | async-start | bytes 4718592 | tf_op jit(solution)/shard_map/reduce_scatter | solution.py:21
  77.2 234.8 %all-gather.8.cloned.1.call-start = ((), (), s32[]{:S(2)}) async-start(), calls=%async_computation.7 | async-start | bytes 4456448 | tf_op jit(solution)/shard_map/all_gather | solution.py:22
  147.1 281.3 %all-gather.6.cloned.1.call-start = ((), (), s32[]{:S(2)}) async-start(), calls=%async_computation.5 | async-start | bytes 4718592 | tf_op jit(solution)/shard_map/all_gather | solution.py:22
  321.3 37.4 %all-to-all-start = ((bf16[8,128,1024]{2,1,0:T(8,128)(2,1)}), bf16[8,128,1024]{2,1,0:T(8,128)(2,1)S(1)}, u32[]{:S(2)}, u32[]{:S(2)}) async-start(bf16[8,128,1024]{2,1,0:T(8,128)(2,1)} %bitcast.81), calls=%async_computation.2 | async-start | bytes 4194304 | tf_op jit(solution)/shard_map/all_to_all | solution.py:33
Sparse Core Ops, SparseCore 0:
  11.0 54.2 all-gather.3
  69.3 77.7 reduce-scatter.4
  150.1 105.3 reduce-scatter.2
  257.8 54.1 all-gather.7
  313.4 114.9 all-gather.5
where the time goes:
time: 461 us; the launch traced here: 453 us
  waiting for transfers between devices  382 us (83%)
  matrix products  27.4 us (6%)
  other arithmetic  21.3 us (5%)
  between operations  13.8 us (3%)
  starting transfers between devices  5.35 us (1%)
    reduce_scatter x2, waiting for transfers between devices, broadcast_by_parts(): own = lax.psum_scatter(padded, axis, scatter_dimension=0, tiled=True)  178 us
    all_gather x2, waiting for transfers between devices, broadcast_by_parts(): lax.all_gather(own, axis, axis=0, tiled=True)[:len(lines)].reshape(x.shape)  125 us
    all_gather x1, waiting for transfers between devices, body(): lax.all_gather(u_rows.astype(jnp.bfloat16), 'mp', axis=0, tiled=True)  46.3 us
    all_to_all x1, waiting for transfers between devices, summed_on_arrival(): lax.all_to_all(pieces, axis, split_axis=0, concat_axis=0, tiled=True)  32.2 us
    dot_general x1, matrix products, body(): jnp.dot(errors, factors, precision=lax.Precision.HIGHEST)  18 us
    dot_general x1, matrix products, body(): lax.dot_general(window, features, (((0,), (0,)), ((), ())), preferred_ele...  9.36 us
  transfers between devices with their start and end apart: 6, of which 6 were waited for; matrix products, arithmetic and copies ran while one was open for 7% of the time, Pallas kernels for 0%

commit v1 on v0

v1 whole, which is shorter than its diff:
```python
import jax
import jax.numpy as jnp
from jax import lax
from jax.experimental import pallas as pl
from jax.experimental.pallas import tpu as pltpu
from jax.sharding import PartitionSpec as P

B = 512
PANELS = 2
WIN = 1024
TOKENS = 16384
HALF = WIN // 2
CORNER = HALF
LOCAL_COLS = 2048
GATHER_COLS = CORNER + LOCAL_COLS
STEPS = 16
PAIR_OFFSETS = (2, 1, 3, 0)
CROSS_AT = (3, 2, 1, 0)
MESH = pl.DeviceIdType.MESH
EXACT = lax.Precision.HIGHEST


def pruned_positions(keep_pairs):
    first, second = keep_pairs[..., 0], keep_pairs[..., 1]
    low = jnp.where(first != 0, 0, jnp.where(second != 1, 1, 2))
    high = jnp.where(second != 3, 3, jnp.where(first != 2, 2, 1))
    both = jnp.stack([low, high], axis=-1).reshape(WIN // 4, 2)
    return (both + 4 * jnp.arange(WIN // 4, dtype=jnp.int32)[:, None]).reshape(HALF)


def keep_columns(pairs):
    positions = jnp.arange(4, dtype=jnp.int32)
    selected = (pairs[:, 0:1] == positions) | (pairs[:, 1:2] == positions)
    return selected.astype(jnp.float32).reshape(-1)


def iota(shape, dim):
    return lax.broadcasted_iota(jnp.int32, shape, dim)


def kernel(
    feat_hbm, w_hbm, u_hbm, lane_idx, row_idx, mask_ref, out_hbm, hess_hbm,
    feat, feat_t, win, acc, sums, relay, from_left, from_right, from_pair,
    wv, uv, ug, wcs, wcb, ev, tri, inv, hout,
    local_sem, win_sem, send_sem, recv_sem,
):
    dp, mp = lax.axis_index("dp"), lax.axis_index("mp")
    x, l = lax.div(dp, 2), lax.rem(dp, 2)
    z, h, k = lax.div(mp, 4), lax.rem(lax.div(mp, 2), 2), lax.rem(mp, 2)
    way = 1 - 2 * k
    r = lax.rem(z * way + 4, 4)
    is_source = mp == 0
    is_owner = dp == 0

    def at_mp(zz, hh, kk):
        return (dp, lax.rem(zz + 8, 4) * 4 + hh * 2 + kk)

    def at_dp(xx, ll):
        return (lax.rem(xx + 8, 4) * 2 + ll, mp)

    pending = []
    count = {"send": 0, "recv": 0}

    def take(kind):
        count[kind] += 1
        return count[kind] - 1

    def remote(src, dst, sent, landed, device):
        return pltpu.make_async_remote_copy(
            src_ref=src, dst_ref=dst, send_sem=send_sem.at[sent], recv_sem=recv_sem.at[landed],
            device_id=device, device_id_type=MESH,
        )

    def guarded(when, run):
        if when is None:
            run()
        else:
            pl.when(when)(run)

    def send(src, dst, landed, device, when=None):
        sent = take("send")
        guarded(when, lambda: remote(src, dst, sent, landed, device).start())
        pending.append((when, src, dst, sent, landed, device))

    def arrived(dst, landed, when=None):
        guarded(when, lambda: remote(dst, dst, 0, landed, at_mp(z, h, 1 - k)).wait_recv())

    load_u = pltpu.make_async_copy(u_hbm, uv, local_sem.at[0])
    load_f = pltpu.make_async_copy(feat_hbm, feat, local_sem.at[1])
    load_w = pltpu.make_async_copy(w_hbm, wv, local_sem.at[2])
    load_u.start()

    def window_block(i):
        t, tq = divmod(i, 4)
        column = pl.multiple_of(lax.rem(x + PAIR_OFFSETS[t], 4) * 256, 256)
        return pltpu.make_async_copy(
            feat_hbm.at[pl.ds(tq * 512, 512), pl.ds(column, 256)], win.at[t, tq], win_sem.at[i]
        )

    @pl.when(is_source)
    def _():
        for i in range(STEPS):
            window_block(i).start()

    load_f.start()
    load_w.start()

    barrier = pltpu.get_barrier_semaphore()
    peers = [(lax.rem(dp + o, 8), mp) for o in range(1, 8)]
    peers += [at_mp(z + 1, h, k), at_mp(z - 1, h, k), at_mp(z, 1 - h, k), at_mp(z, h, 1 - k)]
    for peer in peers:
        pl.semaphore_signal(barrier, inc=1, device_id=peer, device_id_type=MESH)

    load_u.wait()
    picked_rows = (iota((32, 64), 1) + 64 * mp) == row_idx[pl.ds(pl.multiple_of(mp * 32, 32), 32), :]
    picked = jnp.dot(
        picked_rows.astype(jnp.bfloat16), uv[...].astype(jnp.bfloat16), preferred_element_type=jnp.float32
    ).astype(jnp.bfloat16)
    ug[z, h, k, :, CORNER:] = picked

    def column_pick(c):
        wanted = lane_idx[:, c * 128 : (c + 1) * 128]
        return ((iota((256, 128), 0) + 256 * c) == wanted).astype(jnp.bfloat16)

    @pl.when(is_owner)
    def _():
        for c in range(4):
            ug[z, h, k, :, c * 128 : (c + 1) * 128] = jnp.dot(
                picked[:, c * 256 : (c + 1) * 256], column_pick(c), preferred_element_type=jnp.float32
            ).astype(jnp.bfloat16)

    pl.semaphore_wait(barrier, len(peers))

    own_landed = [take("recv") for _ in range(STEPS)]
    partner_landed = [take("recv") for _ in range(STEPS)]

    def piece(i, half):
        t, tq = divmod(i, 4)
        return win.at[t, tq, :, pl.ds(pl.multiple_of(half * 128, 128), 128)]

    def relay_piece(i):
        q = CROSS_AT[i // 4]

        @pl.when(is_source)
        def _():
            window_block(i).wait()

        own = piece(i, k)
        arrived(own, own_landed[i], when=jnp.logical_not(is_source))
        on_first = h == 0
        forward = (on_first & (r < 3)) | ((h == 1) & ((r == q) | (r == (q + 1) % 4)))
        send(own, own, own_landed[i], at_mp(z + way, h, k), when=forward)
        send(own, own, own_landed[i], at_mp(z, 1, k), when=on_first & (r == q))
        send(own, own, own_landed[i], at_mp(z - way, h, k), when=(h == 1) & (r == q))
        other = piece(i, 1 - k)
        send(other, other, own_landed[i], at_mp(z, h, 1 - k), when=is_source)
        send(own, own, partner_landed[i], at_mp(z, h, 1 - k), when=mp != 1)
        return lambda: arrived(other, partner_landed[i], when=jnp.logical_not(is_source))

    corner_landed = take("recv")
    corner = ug.at[z, h, k, :, pl.ds(0, CORNER)]
    for o in range(1, 8):
        send(corner, corner, corner_landed, (lax.rem(dp + o, 8), mp), when=is_owner)

    part_landed = take("recv")
    load_w.wait()

    @pl.when(is_owner)
    def _():
        for c in range(4):
            wcs[:, c * 128 : (c + 1) * 128] = jnp.dot(
                wv[:, c * 256 : (c + 1) * 256], column_pick(c), preferred_element_type=jnp.float32
            ).astype(jnp.bfloat16)
        wcb[0, 0] = wcs[0:128, :]

    for o in range(1, 8):
        send(
            wcs.at[pl.ds(o * 128, 128), :], wcb.at[o // 2, o % 2], part_landed, (jnp.int32(o), mp), when=is_owner
        )

    load_f.wait()

    @pl.loop(0, 8)
    def _(tb):
        block = feat[pl.ds(pl.multiple_of(tb * 256, 256), 256), :]
        feat_t[lax.div(tb, 2), :, pl.ds(pl.multiple_of(lax.rem(tb, 2) * 256, 256), 256)] = block.T

    arrived(corner, corner_landed, when=jnp.logical_not(is_owner))

    class Gather:
        def __init__(self, view, both, pos, line, device):
            self.view, self.both, self.pos, self.line, self.device = view, both, pos, line, device
            self.landed = [take("recv") for _ in range(5)]
            self.after = lax.rem(pos + 1, 4)
            self.before = lax.rem(pos + 3, 4)
            self.far = lax.rem(pos + 2, 4)

        def first(self):
            own = self.view(self.pos, self.line)
            send(own, own, self.landed[0], self.device(self.pos, 1 - self.line))

        def second(self):
            arrived(self.view(self.pos, 1 - self.line), self.landed[0])
            own = self.both(self.pos)
            send(own, own, self.landed[1], self.device(self.pos + 1, self.line))
            send(own, own, self.landed[2], self.device(self.pos - 1, self.line))

        def third(self):
            arrived(self.both(self.before), self.landed[1])
            arrived(self.both(self.after), self.landed[2])
            up, down = self.view(self.before, 0), self.view(self.after, 1)
            send(up, up, self.landed[3], self.device(self.pos + 1, self.line))
            send(down, down, self.landed[4], self.device(self.pos - 1, self.line))

        def finish(self):
            arrived(self.view(self.far, 0), self.landed[3])
            arrived(self.view(self.far, 1), self.landed[4])

    u_gather = Gather(
        lambda p, q: ug.at[p, q, k], lambda p: ug.at[p, :, k], z, h, lambda p, q: at_mp(p, q, k)
    )
    w_gather = Gather(lambda p, q: wcb.at[p, q], lambda p: wcb.at[p], x, l, at_dp)
    plane_landed = take("recv")

    def finish_u():
        u_gather.finish()
        plane = ug.at[:, :, k]
        send(plane, plane, plane_landed, at_mp(z, h, 1 - k))

    def start_w():
        arrived(wcb.at[x, l], part_landed, when=jnp.logical_not(is_owner))
        w_gather.first()

    u_gather.first()
    hooks = {
        2: u_gather.second, 6: u_gather.third, 11: finish_u,
        4: start_w, 7: w_gather.second, 10: w_gather.third, 14: w_gather.finish,
    }

    relay_landed, left_landed, right_landed, pair_landed = (take("recv") for _ in range(4))

    def add_to_acc(source):
        @pl.loop(0, 4)
        def _(m):
            rows = pl.ds(pl.multiple_of(m * 256, 256), 256)
            acc[rows, :] += source[rows, :].astype(jnp.float32)

    def round_acc(slot):
        @pl.loop(0, 4)
        def _(m):
            rows = pl.ds(pl.multiple_of(m * 256, 256), 256)
            sums[slot, rows, :] = acc[rows, :].astype(jnp.bfloat16)

    def reduce_pair(t):
        if t == 0:
            round_acc(0)
            send(sums.at[0], relay, relay_landed, at_dp(x + way, l))
        elif t == 1:
            @pl.when(k == 0)
            def _():
                arrived(relay, relay_landed)
                add_to_acc(relay)

            round_acc(1)
            send(sums.at[1], from_left, left_landed, at_dp(x + 1, l))
        elif t == 2:
            @pl.when(k == 1)
            def _():
                arrived(relay, relay_landed)
                add_to_acc(relay)

            round_acc(2)
            send(sums.at[2], from_right, right_landed, at_dp(x - 1, l))
        else:
            arrived(from_left, left_landed)
            arrived(from_right, right_landed)
            add_to_acc(from_left)
            add_to_acc(from_right)
            mine = pl.ds(pl.multiple_of(l * 128, 128), 128)
            theirs = pl.ds(pl.multiple_of((1 - l) * 128, 128), 128)
            sums[3, :, 0:128] = acc[:, theirs].astype(jnp.bfloat16)
            send(sums.at[3, :, pl.ds(0, 128)], from_pair, pair_landed, at_dp(x, 1 - l))
            return mine

    for i in range(STEPS):
        t, tq = divmod(i, 4)
        partner_here = relay_piece(i)
        if i in hooks:
            hooks[i]()
        partner_here()

        @pl.loop(0, 2)
        def _(m):
            rows = pl.ds(pl.multiple_of(m * 512, 512), 512)
            product = jnp.dot(feat_t[tq, rows, :], win[t, tq], preferred_element_type=jnp.float32)
            if tq == 0:
                acc[rows, :] = product
            else:
                acc[rows, :] += product

        if tq == 3:
            mine = reduce_pair(t)

    arrived(ug.at[:, :, 1 - k], plane_landed)
    tri[...] = ug[:, :, :, :, 0:CORNER].reshape(HALF, CORNER).astype(jnp.float32)
    row, col = iota((128, 128), 0), iota((128, 128), 1)
    inverses = []
    for j in range(4):
        block = tri[j * 128 : (j + 1) * 128, j * 128 : (j + 1) * 128]
        inverses.append(jnp.where(row == col, 1.0 / jnp.where(row == col, block, 1.0), 0.0))
    for level in range(7):
        for j in range(4):
            block = tri[j * 128 : (j + 1) * 128, j * 128 : (j + 1) * 128]
            upper_part = ((row >> level) + 1 == (col >> level)) & ((row >> (level + 1)) == (col >> (level + 1)))
            step = jnp.dot(jnp.where(upper_part, block, 0.0), inverses[j], precision=EXACT)
            inverses[j] = inverses[j] - jnp.dot(inverses[j], step, precision=EXACT)
    for j in range(4):
        inv[j] = inverses[j]

    @pl.loop(0, 8)
    def _(m):
        solved = []
        for j in range(4):
            rest = wcb[lax.div(m, 2), lax.rem(m, 2), :, j * 128 : (j + 1) * 128].astype(jnp.float32)
            for e in range(j):
                rest -= jnp.dot(
                    solved[e], tri[e * 128 : (e + 1) * 128, j * 128 : (j + 1) * 128], precision=EXACT
                )
            solved.append(jnp.dot(rest, inv[j], precision=EXACT))
            ev[pl.ds(pl.multiple_of(m * 128, 128), 128), j * 128 : (j + 1) * 128] = solved[j].astype(jnp.bfloat16)

    @pl.loop(0, 8)
    def _(c):
        cols = pl.ds(pl.multiple_of(c * 256, 256), 256)
        factor = ug[:, :, :, :, pl.ds(pl.multiple_of(c * 256 + CORNER, 256), 256)].reshape(HALF, 256)
        change = jnp.dot(ev[...], factor, preferred_element_type=jnp.float32)
        wv[:, cols] = ((wv[:, cols].astype(jnp.float32) - change) * mask_ref[:, cols]).astype(jnp.bfloat16)

    store_w = pltpu.make_async_copy(wv, out_hbm, local_sem.at[0])
    store_w.start()

    arrived(from_pair, pair_landed)
    total = (acc[:, mine] + from_pair[...].astype(jnp.float32)) * (2.0 / TOKENS)
    hout[...] = total.T
    store_h = pltpu.make_async_copy(hout, hess_hbm, local_sem.at[1])
    store_h.start()

    for when, src, dst, sent, landed, device in pending:
        guarded(when, lambda: remote(src, dst, sent, landed, device).wait_send())
    store_w.wait()
    store_h.wait()


def body(features, weights, u_rows, keep_pairs):
    pruned = pruned_positions(keep_pairs)
    keep = jnp.concatenate([keep_columns(keep_pairs[panel]) for panel in range(PANELS)])
    mask = jnp.concatenate([keep, jnp.ones((LOCAL_COLS - WIN,), jnp.float32)])
    mask = jnp.where(lax.axis_index("dp") == 0, mask, 1.0)[None, :]
    bf16, f32 = jnp.bfloat16, jnp.float32
    anywhere = pl.BlockSpec(memory_space=pl.ANY)
    vmem = pl.BlockSpec(memory_space=pltpu.VMEM)
    return pl.pallas_call(
        kernel,
        out_shape=(
            jax.ShapeDtypeStruct((1024, LOCAL_COLS), bf16),
            jax.ShapeDtypeStruct((128, 1024), f32),
        ),
        in_specs=[anywhere, anywhere, anywhere, vmem, vmem, vmem],
        out_specs=(anywhere, anywhere),
        scratch_shapes=[
            pltpu.VMEM((2048, 1024), bf16),
            pltpu.VMEM((4, 1024, 512), bf16),
            pltpu.VMEM((4, 4, 512, 256), bf16),
            pltpu.VMEM((1024, 256), f32),
            pltpu.VMEM((4, 1024, 256), bf16),
            pltpu.VMEM((1024, 256), bf16),
            pltpu.VMEM((1024, 256), bf16),
            pltpu.VMEM((1024, 256), bf16),
            pltpu.VMEM((1024, 128), bf16),
            pltpu.VMEM((1024, LOCAL_COLS), bf16),
            pltpu.VMEM((64, LOCAL_COLS), f32),
            pltpu.VMEM((4, 2, 2, 32, GATHER_COLS), bf16),
            pltpu.VMEM((1024, HALF), bf16),
            pltpu.VMEM((4, 2, 128, HALF), bf16),
            pltpu.VMEM((1024, HALF), bf16),
            pltpu.VMEM((HALF, HALF), f32),
            pltpu.VMEM((4, 128, 128), f32),
            pltpu.VMEM((128, 1024), f32),
            pltpu.SemaphoreType.DMA((3,)),
            pltpu.SemaphoreType.DMA((STEPS,)),
            pltpu.SemaphoreType.DMA((128,)),
            pltpu.SemaphoreType.DMA((64,)),
        ],
        compiler_params=pltpu.CompilerParams(
            collective_id=0, has_side_effects=True, vmem_limit_bytes=60 * 1024 * 1024
        ),
    )(features, weights, u_rows, pruned[None, :], pruned[:, None], mask)


def solution(mesh):
    in_specs = (P("dp", "mp"), P("mp", "dp"), P("mp", "dp"), P())
    out_specs = (P("mp", "dp"), P("dp", "mp"))
    return jax.shard_map(body, mesh=mesh, in_specs=in_specs, out_specs=out_specs, check_vma=False)
```

time: 461 us -> 193 us (0.42)
  the two profiles are of different devices: /device:TPU:59 before, /device:TPU:101 now
where the time goes in v1:
time: 193 us
  Pallas kernels  183 us (95%)
  local copies, waits for them, and re-layouts  8.23 us (4%)
    pallas_call x1, Pallas kernels, body(): pl.pallas_call(kernel, out_shape=(jax.ShapeDtypeStruct((1024, LOCAL_COLS)...  183 us
    unnamed x4, local copies, waits for them, and re-layouts  5.64 us

profile of v1, /device:TPU:101, one launch (start us, length us, event | category | flops | bytes accessed | tf_op | source)
XLA Modules:
  0.0 193.2 jit_solution(8437815872551008137)
XLA Ops:
  0.6 0.8 fusion.4
  1.4 0.7 slice_bitcast_fusion.1
  2.1 0.1 fusion.3
  2.2 0.1 reshape.135
  2.3 0.1 fusion.1
  2.5 0.1 reshape.134
  2.6 0.6 broadcast_select_fusion.mask_ref
  3.2 0.1 copy.11
  3.3 0.7 add.30.lane_idx
  4.0 0.8 add.32.row_idx
  4.9 182.7 %shard_map.59 = (bf16[1024,2048]{1,0:T(8,128)(2,1)}, f32[128,1024]{1,0:T(8,128)}) custom-call(bf16[2048,1024]{1,0:T(8,128)(2,1)} %feat_hbm.1, bf16[1024,2048]{1,0:T(8,128)(2,1)} %w_hbm.1, f32[64,2048]{1,0:T(8,128)} %u_hbm.1, s32[1,512]{1,0:T(1,128)} %add.30.lane_idx, s32[512,1]{1,0:T(8,128)} %add.32.row_idx, f32[1,2048]{1,0:T(1,128)} %broadcast_select_fusion.mask_ref), custom_call_target="tpu_custom_call" | custom-call | tf_op jit(solution)/shard_map/pallas_call | solution.py:362
  187.5 0.0 copy-start
  187.6 4.8 %copy.16 = bf16[1024,2048]{1,0:T(8,128)(2,1)} copy(bf16[1024,2048]{1,0:T(8,128)(2,1)} %get-tuple-element.14) | data formatting | bytes 8388608
  192.4 0.0 copy-done
  192.4 0.8 copy.17
  (5 shorter events, 0.0 us)
Async XLA Ops:
  187.5 4.9 %copy-start = (f32[128,1024]{1,0:T(8,128)S(1)}, f32[128,1024]{1,0:T(8,128)}, u32[]{:S(2)}) copy-start(f32[128,1024]{1,0:T(8,128)} %get-tuple-element.15) | copy-start | bytes 1572868

commit v2 on v0

v2 whole, which is shorter than its diff:
```python
import jax
import jax.numpy as jnp
from jax import lax
from jax.experimental import pallas as pl
from jax.experimental.pallas import tpu as pltpu
from jax.sharding import PartitionSpec as P

B = 512
PANELS = 2
WIN = 1024
TOKENS = 16384
HALF = WIN // 2
CORNER = HALF
LOCAL_COLS = 2048
STEPS = 16
LAG = 3
PAIR_OFFSETS = (2, 1, 3, 0)
MESH = pl.DeviceIdType.MESH
EXACT = lax.Precision.HIGHEST


def iota(shape, dim):
    return lax.broadcasted_iota(jnp.int32, shape, dim)


def pruned_of(first, second):
    low = jnp.where(first != 0, 0, jnp.where(second != 1, 1, 2))
    high = jnp.where(second != 3, 3, jnp.where(first != 2, 2, 1))
    return low, high


def pruned_lanes(low, high):
    groups = low.shape[0]
    shape = (groups, 2 * groups)
    group, lane = iota(shape, 0), iota(shape, 1)
    own = jnp.where((lane & 1) == 0, low, high) + 4 * group
    return jnp.sum(jnp.where((lane >> 1) == group, own, 0), axis=0, keepdims=True)


def kept_lanes(low, high):
    groups = low.shape[0]
    shape = (groups, 4 * groups)
    group, lane = iota(shape, 0), iota(shape, 1)
    pruned = ((lane >> 2) == group) & (((lane & 3) == low) | ((lane & 3) == high))
    return 1.0 - jnp.sum(jnp.where(pruned, 1.0, 0.0), axis=0, keepdims=True)


def kernel(
    feat_hbm, w_hbm, u_hbm, pairs_ref, out_hbm, hess_hbm,
    feat, feat_t, win, acc, sums, to_pair, relay, from_left, from_right, from_pair,
    wv, uv, picked_rows, ug, cg, wcs, wcb, ev, parts, halves, inv, mask, picks, low_high, hout,
    local_sem, win_sem, send_sem, recv_sem,
):
    dp, mp = lax.axis_index("dp"), lax.axis_index("mp")
    x, l = lax.div(dp, 2), lax.rem(dp, 2)
    z, h, k = lax.div(mp, 4), lax.rem(lax.div(mp, 2), 2), lax.rem(mp, 2)
    is_source = mp == 0
    is_owner = dp == 0
    f32, bf16 = jnp.float32, jnp.bfloat16

    def at_mp(zz, hh, kk):
        return (dp, lax.rem(zz + 8, 4) * 4 + hh * 2 + kk)

    def at_dp(xx, ll):
        return (lax.rem(xx + 8, 4) * 2 + ll, mp)

    counter = [0]

    def take(n=1):
        counter[0] += n
        return counter[0] - n

    piece_landed = take(2 * STEPS)
    shared_landed = take(2 * STEPS)
    u_landed, c_landed, w_landed = take(5), take(5), take(5)
    picked_landed, corner_landed, part_landed = take(1), take(2), take(2)
    level_landed, inverse_landed, rows_landed = take(4), take(1), take(1)
    relay_landed, left_landed, right_landed, pair_landed = take(1), take(1), take(1), take(1)

    def remote(src, dst, sent, landed, device):
        return pltpu.make_async_remote_copy(
            src_ref=src, dst_ref=dst, send_sem=send_sem.at[sent], recv_sem=recv_sem.at[landed],
            device_id=device, device_id_type=MESH,
        )

    def arrived(dst, landed):
        remote(dst, dst, 0, landed, at_mp(z, h, 1 - k)).wait_recv()

    load_u = pltpu.make_async_copy(u_hbm, uv, local_sem.at[0])
    load_f = pltpu.make_async_copy(feat_hbm, feat, local_sem.at[1])
    load_w = pltpu.make_async_copy(w_hbm, wv, local_sem.at[2])
    load_u.start()

    def window_block(i, half):
        t, tq = divmod(i, 4)
        column = pl.multiple_of(lax.rem(x + PAIR_OFFSETS[t], 4) * 256 + half * 128, 128)
        return pltpu.make_async_copy(
            feat_hbm.at[pl.ds(tq * 512, 512), pl.ds(column, 128)], win.at[t, tq, half], win_sem.at[2 * i + half]
        )

    @pl.when(is_source)
    def _():
        for i in range(STEPS):
            for half in range(2):
                window_block(i, half).start()

    load_w.start()
    load_f.start()

    barrier = pltpu.get_barrier_semaphore()
    peers = [(lax.rem(dp + o, 8), mp) for o in range(1, 8)]
    peers += [(lax.rem(dp + o, 8), mp + 1 - 2 * k) for o in range(1, 8)]
    peers += [at_mp(z + 1, h, k), at_mp(z - 1, h, k), at_mp(z, 1 - h, k), at_mp(z, h, 1 - k)]
    for peer in peers:
        pl.semaphore_signal(barrier, inc=1, device_id=peer, device_id_type=MESH)

    wide = jnp.concatenate([pairs_ref[0], pairs_ref[1], pairs_ref[0], pairs_ref[1]], axis=0).astype(f32)
    tall = wide.T.astype(jnp.int32)
    for panel in range(PANELS):
        low, high = pruned_of(tall[:, 2 * panel : 2 * panel + 1], tall[:, 2 * panel + 1 : 2 * panel + 2])
        low_high[0, panel * 128 : (panel + 1) * 128, :] = low
        low_high[1, panel * 128 : (panel + 1) * 128, :] = high
    for c in range(4):
        low, high = low_high[0, c * 64 : (c + 1) * 64, :], low_high[1, c * 64 : (c + 1) * 64, :]
        picks[c] = (iota((256, 128), 0) == pruned_lanes(low, high)).astype(bf16)
        mask[:, c * 256 : (c + 1) * 256] = jnp.where(is_owner, kept_lanes(low, high), 1.0)

    own_groups = pl.ds(pl.multiple_of(mp * 16, 16), 16)
    own_rows = pruned_lanes(low_high[0, own_groups, :], low_high[1, own_groups, :])
    row_pick = (iota((64, 32), 0) == own_rows).astype(bf16)
    load_u.wait()
    picked = lax.dot_general(
        row_pick, uv[...].astype(bf16), (((0,), (0,)), ((), ())), preferred_element_type=f32
    ).astype(bf16)
    picked_rows[...] = picked

    @pl.when(k == 1)
    def _():
        ug[z, h, 1] = picked


    @pl.when(is_owner)
    def _():
        for c in range(4):
            cg[z, h, k, :, c * 128 : (c + 1) * 128] = jnp.dot(
                picked[:, c * 256 : (c + 1) * 256], picks[c], preferred_element_type=f32
            ).astype(bf16)

    pl.semaphore_wait(barrier, len(peers))

    def pick_weights():
        load_w.wait()

        @pl.when(is_owner)
        def _():
            for c in range(4):
                wcs[:, c * 128 : (c + 1) * 128] = jnp.dot(
                    wv[:, c * 256 : (c + 1) * 256], picks[c], preferred_element_type=f32
                ).astype(bf16)

    def transpose_features():
        load_f.wait()

        @pl.loop(0, 8)
        def _(tb):
            block = feat[pl.ds(pl.multiple_of(tb * 256, 256), 256), :]
            feat_t[lax.div(tb, 2), :, pl.ds(pl.multiple_of(lax.rem(tb, 2) * 256, 256), 256)] = block.T

    def product(i):
        t, tq = divmod(i, 4)

        @pl.loop(0, 2)
        def _(m):
            rows = pl.ds(pl.multiple_of(m * 512, 512), 512)
            columns = jnp.concatenate([win[t, tq, 0], win[t, tq, 1]], axis=1)
            part = jnp.dot(feat_t[tq, rows, :], columns, preferred_element_type=f32)
            if tq == 0:
                acc[t, rows, :] = part
            else:
                acc[t, rows, :] += part

    def add_to(slot, source):
        @pl.loop(0, 4)
        def _(m):
            rows = pl.ds(pl.multiple_of(m * 256, 256), 256)
            acc[slot, rows, :] += source[rows, :].astype(f32)

    def round_sum(slot):
        @pl.loop(0, 4)
        def _(m):
            rows = pl.ds(pl.multiple_of(m * 256, 256), 256)
            sums[slot, rows, :] = acc[slot, rows, :].astype(bf16)

    mine = pl.ds(pl.multiple_of(l * 128, 128), 128)
    theirs = pl.ds(pl.multiple_of((1 - l) * 128, 128), 128)

    def update_columns(c):
        cols = pl.ds(c * 256, 256)
        factor = ug[:, :, :, :, cols].reshape(HALF, 256)
        updated = wv[:, cols].astype(f32) - jnp.dot(ev[...], factor, preferred_element_type=f32)
        if c < 4:
            updated = updated * mask[:, c * 256 : (c + 1) * 256]
        wv[:, cols] = updated.astype(bf16)

    def solve_rows(core):
        @pl.loop(0, 2)
        def _(m):
            lead = wcb[pl.ds(m * 2, 2), :, core].reshape(512, HALF)
            rows = pl.ds(pl.multiple_of(m * 512, 512), 512)
            first = lead[:, 0:256]
            ev[rows, 0:256] = (
                jnp.dot(first, inv[0, 0:256, 0:256], preferred_element_type=f32)
                + jnp.dot(first, inv[1, 0:256, 0:256], preferred_element_type=f32)
            ).astype(bf16)
            ev[rows, 256:] = (
                jnp.dot(lead, inv[0, :, 256:], preferred_element_type=f32)
                + jnp.dot(lead, inv[1, :, 256:], preferred_element_type=f32)
            ).astype(bf16)

    store_w = pltpu.make_async_copy(wv, out_hbm, local_sem.at[0])
    store_h = pltpu.make_async_copy(hout, hess_hbm, local_sem.at[1])

    def run(core):
        way = 1 - 2 * core
        pending = []
        sends = [0]
        partner = at_mp(z, h, 1 - core)

        def send(src, dst, landed, device, when=None):
            sent = sends[0]
            sends[0] += 1
            make = lambda: remote(src, dst, sent, landed, device)
            if when is None:
                make().start()
            else:
                pl.when(when)(lambda: make().start())
            pending.append((when, make))

        def send_right(do_round=True):
            round_sum(1)
            send(sums.at[1], from_left, left_landed, at_dp(x + 1, l))

        def send_left():
            round_sum(2)
            send(sums.at[2], from_right, right_landed, at_dp(x - 1, l))

        def add_relayed(slot):
            arrived(relay, relay_landed)
            add_to(slot, relay)

        def reduce_pairs(i):
            if i == 3:
                round_sum(0)
                send(sums.at[0], relay, relay_landed, at_dp(x + way, l))
            if core == 0:
                if i == 9:
                    add_relayed(1)
                    send_right()
                if i == 11:
                    send_left()
            else:
                if i == 7:
                    send_right()
                if i == 11:
                    add_relayed(2)
                    send_left()

        def reduce_own():
            arrived(from_left, left_landed)
            arrived(from_right, right_landed)
            add_to(3, from_left)
            add_to(3, from_right)
            to_pair[...] = acc[3, :, theirs].astype(bf16)
            send(to_pair, from_pair, pair_landed, at_dp(x, 1 - l))

        def finish_hessian():
            arrived(from_pair, pair_landed)
            total = (acc[3, :, mine] + from_pair[...].astype(f32)) * (2.0 / TOKENS)
            hout[...] = total.T
            store_h.start()

        def send_corner():
            for o in range(7, -1, -1):
                device = (jnp.int32(o), mp + 1 - core)
                if o == 0:
                    if core == 0:
                        send(cg.at[z, h, 0], cg.at[z, h, 0], corner_landed, device, when=is_owner)
                else:
                    send(cg.at[z, h, core], cg.at[z, h, core], corner_landed + core, device, when=is_owner)

        def send_weights():
            pick_weights()
            for o in range(7, -1, -1):
                device = (jnp.int32(o), mp + 1 - core)
                part = wcs.at[pl.ds(o * 128, 128), :]
                target = wcb.at[o // 2, o % 2, core]
                if o == 0:
                    if core == 0:
                        send(part, target, part_landed, device, when=is_owner)
                else:
                    send(part, target, part_landed + core, device, when=is_owner)

        if core == 0:
            late = jnp.where((z == 1) | (z == 3), LAG, 0)
            early_set = jnp.where(z == 3, 1, 0)
            send_base = 0

            def piece(i, half):
                return win.at[lax.div(i, 4), lax.rem(i, 4), half]

            def routes(half):
                step = 1 - 2 * half
                r = lax.rem(z * step + 4, 4)
                on_first = h == 0
                forward = (on_first & (r < 3)) | ((h == 1) & ((r == 1) | (r == 2)))
                cross = on_first & (r == 1)
                back = (h == 1) & (r == 1)
                return (
                    (forward, at_mp(z + step, h, 0), 0),
                    (cross, at_mp(z, 1, 0), 1),
                    (back, at_mp(z - step, h, 0), 2),
                )

            def copies(i, half):
                ref = piece(i, half)
                slot = 2 * i + half
                for when, device, kind in routes(half):
                    yield when, remote(ref, ref, 4 * slot + kind, piece_landed + slot, device)
                yield None, remote(ref, ref, 4 * slot + 3, shared_landed + slot, partner)

            def pass_on(i, half):
                for when, copy in copies(i, half):
                    if when is None:
                        copy.start()
                    else:
                        pl.when(when)(copy.start)

            sends[0] = 8 * STEPS

            def start_pieces(some):
                @pl.when(is_source)
                def _():
                    for i in some:
                        for half in range(2):
                            window_block(i, half).wait()
                            pass_on(i, half)

            send_corner()
            send(picked_rows, ug.at[z, h, 0], picked_landed, partner)
            start_pieces(range(4))
            send_weights()
            start_pieces(range(4, STEPS))
            transpose_features()

            def take_piece(i, half):
                arrived(piece(i, half), piece_landed + 2 * i + half)
                pass_on(i, half)

            for step in range(STEPS + LAG):
                if step < STEPS:
                    pl.when(jnp.logical_not(is_source))(lambda: take_piece(step, early_set))
                index = step - late
                ready = jnp.logical_not(is_source) & (index >= 0) & (index < STEPS)
                pl.when(ready)(lambda: take_piece(index, 1 - early_set))
                i = step - LAG
                if i >= 0:
                    product(i)
                    reduce_pairs(i)

            reduce_own()
            arrived(inv, inverse_landed)
            arrived(wcb.at[:, :, 0], rows_landed)
            solve_rows(0)
            for n, zz in enumerate((z, z + 3, z + 1, z + 2)):
                arrived(ug.at[lax.rem(zz, 4)], level_landed + n)
            for c in range(8):
                update_columns(c)
            store_w.start()
            finish_hessian()
            for i in range(STEPS):
                for half in range(2):
                    for when, copy in copies(jnp.int32(i), half):
                        if when is None:
                            copy.wait_send()
                        else:
                            pl.when(when)(copy.wait_send)
        else:

            class Gather:
                def __init__(self, buffer, landed, pos, line, device):
                    self.buffer, self.pos, self.line, self.device = buffer, pos, line, device
                    self.landed = landed
                    self.after = lax.rem(pos + 1, 4)
                    self.before = lax.rem(pos + 3, 4)
                    self.far = lax.rem(pos + 2, 4)

                def move(self, view, n, device):
                    send(view, view, self.landed + n, device)

                def first(self):
                    self.move(self.buffer.at[self.pos, self.line], 0, self.device(self.pos, 1 - self.line))

                def second(self):
                    arrived(self.buffer.at[self.pos, 1 - self.line], self.landed)
                    own = self.buffer.at[self.pos]
                    self.move(own, 1, self.device(self.pos + 1, self.line))
                    self.move(own, 2, self.device(self.pos - 1, self.line))

                def third(self):
                    arrived(self.buffer.at[self.before], self.landed + 1)
                    arrived(self.buffer.at[self.after], self.landed + 2)
                    self.move(self.buffer.at[self.before, 0], 3, self.device(self.pos + 1, self.line))
                    self.move(self.buffer.at[self.after, 1], 4, self.device(self.pos - 1, self.line))

                def finish(self):
                    arrived(self.buffer.at[self.far, 0], self.landed + 3)
                    arrived(self.buffer.at[self.far, 1], self.landed + 4)

            over_mp = lambda p, q: at_mp(p, q, 1)
            u_gather = Gather(ug, u_landed, z, h, over_mp)
            c_gather = Gather(cg, c_landed, z, h, over_mp)
            w_gather = Gather(wcb, w_landed, x, l, at_dp)
            levels = (u_gather.pos, u_gather.before, u_gather.after, u_gather.far)

            def share_level(n):
                send(ug.at[levels[n]], ug.at[levels[n]], level_landed + n, partner)

            row, col = iota((128, 128), 0), iota((128, 128), 1)

            def system(i, j, rows, cols):
                view = cg[i : i + rows // 128, :, :, :, j * 128 : j * 128 + cols]
                return view.reshape(rows, cols).astype(f32)

            def exact_dot(a, b):
                return jnp.dot(a, b, precision=EXACT)

            def invert_diagonal():
                for j in range(4):
                    block = system(j, j, 128, 128)
                    parts[j] = jnp.where(row == col, 1.0 / jnp.where(row == col, block, 1.0), 0.0)

            def invert_level(level):
                same = (row >> (level + 1)) == (col >> (level + 1))
                upper_part = ((row >> level) + 1 == (col >> level)) & same
                steps = [exact_dot(jnp.where(upper_part, system(j, j, 128, 128), 0.0), parts[j]) for j in range(4)]
                for j in range(4):
                    parts[j] = parts[j] - exact_dot(parts[j], steps[j])

            def invert_halves():
                for j in range(2):
                    low, high = parts[2 * j], parts[2 * j + 1]
                    halves[j, 0:128, 0:128] = low
                    halves[j, 128:, 128:] = high
                    halves[j, 128:, 0:128] = jnp.zeros((128, 128), f32)
                    halves[j, 0:128, 128:] = -exact_dot(low, exact_dot(system(2 * j, 2 * j + 1, 128, 128), high))

            def keep_split(part, rows, cols):
                rounded = part.astype(bf16)
                inv[0, rows : rows + 256, cols : cols + 256] = rounded
                inv[1, rows : rows + 256, cols : cols + 256] = (part - rounded.astype(f32)).astype(bf16)

            def invert_whole():
                keep_split(halves[0], 0, 0)
                keep_split(halves[1], 256, 256)
                keep_split(-exact_dot(halves[0], exact_dot(system(0, 2, 256, 256), halves[1])), 0, 256)
                for n in range(2):
                    inv[n, 256:, 0:256] = jnp.zeros((256, 256), bf16)
                send(inv, inv, inverse_landed, partner)

            def consume(i):
                for half in range(2):
                    arrived(win.at[i // 4, i % 4, half], shared_landed + 2 * i + half)
                product(i)
                reduce_pairs(i)

            def start_u():
                arrived(ug.at[z, h, 0], picked_landed)
                u_gather.first()

            def start_c():
                arrived(cg.at[z, h, 0], corner_landed)
                pl.when(jnp.logical_not(is_owner))(lambda: arrived(cg.at[z, h, 1], corner_landed + 1))
                c_gather.first()

            def start_w():
                @pl.when(is_owner)
                def _():
                    wcb[0, 0, 1] = wcs[0:128, :]

                arrived(wcb.at[x, l, 0], part_landed)
                pl.when(jnp.logical_not(is_owner))(lambda: arrived(wcb.at[x, l, 1], part_landed + 1))
                w_gather.first()

            def third_u():
                u_gather.third()
                for n in range(3):
                    share_level(n)

            def finish_u():
                u_gather.finish()
                share_level(3)

            def finish_w():
                w_gather.finish()
                send(wcb.at[:, :, 0], wcb.at[:, :, 0], rows_landed, partner)

            send_corner()
            start_u()
            send_weights()
            start_c()
            transpose_features()
            c_gather.second()
            c_gather.third()
            u_gather.second()
            start_w()
            c_gather.finish()
            invert_diagonal()
            for n in range(3):
                invert_level(n)
            w_gather.second()
            for n in range(3, 7):
                invert_level(n)
            invert_halves()
            invert_whole()
            third_u()
            consume(0)
            consume(1)
            w_gather.third()
            consume(2)
            consume(3)
            finish_u()
            consume(4)
            consume(5)
            finish_w()
            consume(6)
            consume(7)
            solve_rows(1)
            for i in range(8, STEPS):
                update_columns(i - 8)
                consume(i)
            store_w.start()
            reduce_own()
            finish_hessian()

        for when, make in pending:
            if when is None:
                make().wait_send()
            else:
                pl.when(when)(lambda: make().wait_send())
        store_w.wait()
        store_h.wait()

    pl.when(k == 0)(lambda: run(0))
    pl.when(k == 1)(lambda: run(1))


def body(features, weights, u_rows, keep_pairs):
    bf16, f32 = jnp.bfloat16, jnp.float32
    anywhere = pl.BlockSpec(memory_space=pl.ANY)
    vmem = pl.BlockSpec(memory_space=pltpu.VMEM)
    return pl.pallas_call(
        kernel,
        out_shape=(
            jax.ShapeDtypeStruct((1024, LOCAL_COLS), bf16),
            jax.ShapeDtypeStruct((128, 1024), f32),
        ),
        in_specs=[anywhere, anywhere, anywhere, vmem],
        out_specs=(anywhere, anywhere),
        scratch_shapes=[
            pltpu.VMEM((2048, 1024), bf16),
            pltpu.VMEM((4, 1024, 512), bf16),
            pltpu.VMEM((4, 4, 2, 512, 128), bf16),
            pltpu.VMEM((4, 1024, 256), f32),
            pltpu.VMEM((3, 1024, 256), bf16),
            pltpu.VMEM((1024, 128), bf16),
            pltpu.VMEM((1024, 256), bf16),
            pltpu.VMEM((1024, 256), bf16),
            pltpu.VMEM((1024, 256), bf16),
            pltpu.VMEM((1024, 128), bf16),
            pltpu.VMEM((1024, LOCAL_COLS), bf16),
            pltpu.VMEM((64, LOCAL_COLS), f32),
            pltpu.VMEM((32, LOCAL_COLS), bf16),
            pltpu.VMEM((4, 2, 2, 32, LOCAL_COLS), bf16),
            pltpu.VMEM((4, 2, 2, 32, CORNER), bf16),
            pltpu.VMEM((1024, HALF), bf16),
            pltpu.VMEM((4, 2, 2, 128, HALF), bf16),
            pltpu.VMEM((1024, HALF), bf16),
            pltpu.VMEM((4, 128, 128), f32),
            pltpu.VMEM((2, 256, 256), f32),
            pltpu.VMEM((2, HALF, HALF), bf16),
            pltpu.VMEM((1, WIN), f32),
            pltpu.VMEM((4, 256, 128), bf16),
            pltpu.VMEM((2, 256, 1), jnp.int32),
            pltpu.VMEM((128, 1024), f32),
            pltpu.SemaphoreType.DMA((3,)),
            pltpu.SemaphoreType.DMA((2 * STEPS,)),
            pltpu.SemaphoreType.DMA((192,)),
            pltpu.SemaphoreType.DMA((112,)),
        ],
        compiler_params=pltpu.CompilerParams(
            collective_id=0, has_side_effects=True, vmem_limit_bytes=60 * 1024 * 1024
        ),
    )(features, weights, u_rows, keep_pairs.transpose(0, 2, 1))


def solution(mesh):
    in_specs = (P("dp", "mp"), P("mp", "dp"), P("mp", "dp"), P())
    out_specs = (P("mp", "dp"), P("dp", "mp"))
    return jax.shard_map(body, mesh=mesh, in_specs=in_specs, out_specs=out_specs, check_vma=False)
```

time: 461 us -> 85.9 us (0.19); the launches traced: 453 us -> 85.8 us
  waiting for transfers between devices: 382 us -> 0 us
  Pallas kernels: 0 us -> 79.5 us
  matrix products: 27.4 us -> 0 us
  other arithmetic: 21.3 us -> 0 us
  between operations: 13.8 us -> 0.65 us
  starting transfers between devices: 5.35 us -> 0 us
    reduce_scatter x2 -> x0, waiting for transfers between devices: 178 us -> none  [broadcast_by_parts(): own = lax.psum_scatter(padded, axis, scatter_dimension=0, tiled=True)]
    all_gather x3 -> x0, waiting for transfers between devices: 171 us -> none  [the longest x2 125 us: broadcast_by_parts(): lax.all_gather(own, axis, axis=0, tiled=True)[:len(lines)].reshape(x.shape)]
    pallas_call x0 -> x1, Pallas kernels: none -> 79.5 us  [body(): pl.pallas_call(kernel, out_shape=(jax.ShapeDtypeStruct((1024, LOCAL_COLS)...]
    all_to_all x1 -> x0, waiting for transfers between devices: 32.2 us -> none  [summed_on_arrival(): lax.all_to_all(pieces, axis, split_axis=0, concat_axis=0, tiled=True)]
    dot_general x2 -> x0, matrix products: 27.4 us -> none  [the longest x1 18 us: body(): jnp.dot(errors, factors, precision=lax.Precision.HIGHEST)]
    convert_element_type x5 -> x0, other arithmetic: 15 us -> none  [the longest x1 6.5 us: body(): lax.all_gather(u_rows.astype(jnp.bfloat16), 'mp', axis=0, tiled=True)]
    all_to_all x1 -> x0, starting transfers between devices: 5.15 us -> none  [summed_on_arrival(): lax.all_to_all(pieces, axis, split_axis=0, concat_axis=0, tiled=True)]
    select_n x3 -> x0, other arithmetic: 5.12 us -> none  [the longest x2 5.11 us: broadcast_by_parts(): jnp.where(lax.axis_index(axis) == root, x, jnp.zeros_like(x))]
  transfers between devices with their start and end apart: 6 -> 0, of which waited for: 6 -> 0; matrix products, arithmetic and copies ran while one was open for 7% -> 0% of each run, Pallas kernels for 0% -> 0%
where the time goes in v2:
time: 85.9 us; the launch traced here: 85.8 us
  Pallas kernels  79.5 us (93%)
  local copies, waits for them, and re-layouts  5.64 us (7%)
    pallas_call x1, Pallas kernels, body(): pl.pallas_call(kernel, out_shape=(jax.ShapeDtypeStruct((1024, LOCAL_COLS)...  79.5 us
    unnamed x4, local copies, waits for them, and re-layouts  5.64 us

profile of v2, /device:TPU:59, one launch (start us, length us, event | category | flops | bytes accessed | tf_op | source)
XLA Modules:
  0.0 85.8 jit_solution(17545781480309361123)
XLA Ops:
  0.6 79.5 %shard_map.59 = (bf16[1024,2048]{1,0:T(8,128)(2,1)}, f32[128,1024]{1,0:T(8,128)}) custom-call(bf16[2048,1024]{1,0:T(8,128)(2,1)} %feat_hbm.1, bf16[1024,2048]{1,0:T(8,128)(2,1)} %w_hbm.1, f32[64,2048]{1,0:T(8,128)} %u_hbm.1, s32[2,2,128]{2,1,0:T(2,128)} %bitcast.1), custom_call_target="tpu_custom_call" | custom-call | tf_op jit(solution)/shard_map/pallas_call | solution.py:561
  80.1 0.0 copy-start
  80.2 4.8 %copy.8 = bf16[1024,2048]{1,0:T(8,128)(2,1)} copy(bf16[1024,2048]{1,0:T(8,128)(2,1)} %get-tuple-element.4) | data formatting | bytes 8388608
  85.0 0.0 copy-done
  85.0 0.8 copy.9
Async XLA Ops:
  80.1 4.9 %copy-start = (f32[128,1024]{1,0:T(8,128)S(1)}, f32[128,1024]{1,0:T(8,128)}, u32[]{:S(2)}) copy-start(f32[128,1024]{1,0:T(8,128)} %get-tuple-element.5) | copy-start | bytes 1572868

commit v3 on v2

--- a/solution.py
+++ b/solution.py
@@ -13,8 +13,7 @@
 CORNER = HALF
 LOCAL_COLS = 2048
 STEPS = 16
-LAG = 3
-PAIR_OFFSETS = (2, 1, 3, 0)
+LAG = 6
 MESH = pl.DeviceIdType.MESH
 EXACT = lax.Precision.HIGHEST
 
@@ -75,7 +74,7 @@
     u_landed, c_landed, w_landed = take(5), take(5), take(5)
     picked_landed, corner_landed, part_landed = take(1), take(2), take(2)
     level_landed, inverse_landed, rows_landed = take(4), take(1), take(1)
-    relay_landed, left_landed, right_landed, pair_landed = take(1), take(1), take(1), take(1)
+    relay_landed, left_landed, right_landed, pair_landed = take(1), take(2), take(2), take(1)
 
     def remote(src, dst, sent, landed, device):
         return pltpu.make_async_remote_copy(
@@ -93,7 +92,11 @@
 
     def window_block(i, half):
         t, tq = divmod(i, 4)
-        column = pl.multiple_of(lax.rem(x + PAIR_OFFSETS[t], 4) * 256 + half * 128, 128)
+        if t == 0 or t == 3:
+            owner = lax.rem(x + (2 if t == 0 else 0), 4) * 2 + (l if half else 1 - l)
+        else:
+            owner = lax.rem(x + (3 if half else 1), 4) * 2 + (1 - l if t == 1 else l)
+        column = pl.multiple_of(owner * 128, 128)
         return pltpu.make_async_copy(
             feat_hbm.at[pl.ds(tq * 512, 512), pl.ds(column, 128)], win.at[t, tq, half], win_sem.at[2 * i + half]
         )
@@ -179,20 +182,21 @@
             else:
                 acc[t, rows, :] += part
 
-    def add_to(slot, source):
+    def add_to(slot, half, source):
+        cols = pl.ds(half * 128, 128)
+
         @pl.loop(0, 4)
         def _(m):
             rows = pl.ds(pl.multiple_of(m * 256, 256), 256)
-            acc[slot, rows, :] += source[rows, :].astype(f32)
-
-    def round_sum(slot):
+            acc[slot, rows, cols] += source[rows, :].astype(f32)
+
+    def round_sum(slot, half):
+        cols = pl.ds(half * 128, 128)
+
         @pl.loop(0, 4)
         def _(m):
             rows = pl.ds(pl.multiple_of(m * 256, 256), 256)
-            sums[slot, rows, :] = acc[slot, rows, :].astype(bf16)
-
-    mine = pl.ds(pl.multiple_of(l * 128, 128), 128)
-    theirs = pl.ds(pl.multiple_of((1 - l) * 128, 128), 128)
+            sums[slot, half, rows, :] = acc[slot, rows, cols].astype(bf16)
 
     def update_columns(c):
         cols = pl.ds(c * 256, 256)
@@ -236,47 +240,43 @@
                 pl.when(when)(lambda: make().start())
             pending.append((when, make))
 
-        def send_right(do_round=True):
-            round_sum(1)
-            send(sums.at[1], from_left, left_landed, at_dp(x + 1, l))
-
-        def send_left():
-            round_sum(2)
-            send(sums.at[2], from_right, right_landed, at_dp(x - 1, l))
-
-        def add_relayed(slot):
-            arrived(relay, relay_landed)
-            add_to(slot, relay)
+        def send_sum(slot, half):
+            round_sum(slot, half)
+            if half == 0:
+                send(sums.at[slot, 0], from_left.at[slot - 1], left_landed + slot - 1, at_dp(x + 1, l))
+            else:
+                send(sums.at[slot, 1], from_right.at[slot - 1], right_landed + slot - 1, at_dp(x - 1, l))
 
         def reduce_pairs(i):
             if i == 3:
-                round_sum(0)
+                round_sum(0, 0)
+                round_sum(0, 1)
                 send(sums.at[0], relay, relay_landed, at_dp(x + way, l))
-            if core == 0:
-                if i == 9:
-                    add_relayed(1)
-                    send_right()
-                if i == 11:
-                    send_left()
-            else:
-                if i == 7:
-                    send_right()
-                if i == 11:
-                    add_relayed(2)
-                    send_left()
-
-        def reduce_own():
-            arrived(from_left, left_landed)
-            arrived(from_right, right_landed)
-            add_to(3, from_left)
-            add_to(3, from_right)
-            to_pair[...] = acc[3, :, theirs].astype(bf16)
+            if i == 7:
+                send_sum(1, 1 - core)
+            if i == 9:
+                arrived(relay, relay_landed)
+                add_to(1, core, relay.at[0])
+                send_sum(1, core)
+            if i == 11:
+                send_sum(2, 1 - core)
+                add_to(2, core, relay.at[1])
+                send_sum(2, core)
+
+        def own_sum(n):
+            arrived(from_left.at[n], left_landed + n)
+            arrived(from_right.at[n], right_landed + n)
+            total = acc[3, :, n * 128 : (n + 1) * 128] + from_left[n].astype(f32)
+            return total + from_right[n].astype(f32)
+
+        def send_pair():
+            to_pair[...] = own_sum(0).astype(bf16)
             send(to_pair, from_pair, pair_landed, at_dp(x, 1 - l))
 
         def finish_hessian():
+            total = own_sum(1)
             arrived(from_pair, pair_landed)
-            total = (acc[3, :, mine] + from_pair[...].astype(f32)) * (2.0 / TOKENS)
-            hout[...] = total.T
+            hout[...] = ((total + from_pair[...].astype(f32)) * (2.0 / TOKENS)).T
             store_h.start()
 
         def send_corner():
@@ -367,7 +367,7 @@
                     product(i)
                     reduce_pairs(i)
 
-            reduce_own()
+            send_pair()
             arrived(inv, inverse_landed)
             arrived(wcb.at[:, :, 0], rows_landed)
             solve_rows(0)
@@ -514,32 +514,38 @@
             u_gather.second()
             start_w()
             c_gather.finish()
+            consume(0)
             invert_diagonal()
-            for n in range(3):
+            invert_level(0)
+            invert_level(1)
+            w_gather.second()
+            consume(1)
+            invert_level(2)
+            invert_level(3)
+            consume(2)
+            third_u()
+            consume(3)
+            for n in range(4, 7):
                 invert_level(n)
-            w_gather.second()
-            for n in range(3, 7):
-                invert_level(n)
+            w_gather.third()
+            consume(4)
             invert_halves()
+            consume(5)
             invert_whole()
-            third_u()
-            consume(0)
-            consume(1)
-            w_gather.third()
-            consume(2)
-            consume(3)
             finish_u()
-            consume(4)
-            consume(5)
-            finish_w()
             consume(6)
             consume(7)
+            finish_w()
+            consume(8)
+            consume(9)
             solve_rows(1)
-            for i in range(8, STEPS):
-                update_columns(i - 8)
+            for i in range(10, STEPS):
+                update_columns(i - 10)
                 consume(i)
+            send_pair()
+            update_columns(6)
+            update_columns(7)
             store_w.start()
-            reduce_own()
             finish_hessian()
 
         for when, make in pending:
@@ -571,11 +577,11 @@
             pltpu.VMEM((4, 1024, 512), bf16),
             pltpu.VMEM((4, 4, 2, 512, 128), bf16),
             pltpu.VMEM((4, 1024, 256), f32),
-            pltpu.VMEM((3, 1024, 256), bf16),
+            pltpu.VMEM((3, 2, 1024, 128), bf16),
             pltpu.VMEM((1024, 128), bf16),
-            pltpu.VMEM((1024, 256), bf16),
-            pltpu.VMEM((1024, 256), bf16),
-            pltpu.VMEM((1024, 256), bf16),
+            pltpu.VMEM((2, 1024, 128), bf16),
+            pltpu.VMEM((2, 1024, 128), bf16),
+            pltpu.VMEM((2, 1024, 128), bf16),
             pltpu.VMEM((1024, 128), bf16),
             pltpu.VMEM((1024, LOCAL_COLS), bf16),
             pltpu.VMEM((64, LOCAL_COLS), f32),
@@ -598,7 +604,7 @@
             pltpu.SemaphoreType.DMA((112,)),
         ],
         compiler_params=pltpu.CompilerParams(
-            collective_id=0, has_side_effects=True, vmem_limit_bytes=60 * 1024 * 1024
+            collective_id=0, has_side_effects=True, vmem_limit_bytes=47 * 1024 * 1024
         ),
     )(features, weights, u_rows, keep_pairs.transpose(0, 2, 1))
 

time: 85.9 us -> 78.3 us (0.912)
  the two profiles are of different devices: /device:TPU:59 before, /device:TPU:24 now
where the time goes in v3:
time: 78.3 us; the launch traced here: 78.2 us
  Pallas kernels  73 us (93%)
  local copies, waits for them, and re-layouts  4.52 us (6%)
    pallas_call x1, Pallas kernels, body(): pl.pallas_call(kernel, out_shape=(jax.ShapeDtypeStruct((1024, LOCAL_COLS)...  73 us
    unnamed x6, local copies, waits for them, and re-layouts  4.52 us

profile of v3, /device:TPU:24, one launch (start us, length us, event | category | flops | bytes accessed | tf_op | source)
XLA Modules:
  0.0 78.2 jit_solution(15028452292194062759)
XLA Ops:
  0.6 0.0 copy-start
  0.6 1.0 %copy-done = f32[64,2048]{1,0:T(8,128)S(1)} copy-done((f32[64,2048]{1,0:T(8,128)S(1)}, f32[64,2048]{1,0:T(8,128)}, u32[]{:S(2)}) %copy-start) | copy-done | bytes 524312
  1.7 0.0 copy-start.1
  1.7 0.7 copy-done.1
  2.4 73.0 %shard_map.59 = (bf16[1024,2048]{1,0:T(8,128)(2,1)S(1)}, f32[128,1024]{1,0:T(8,128)S(1)}) custom-call(bf16[2048,1024]{1,0:T(8,128)(2,1)} %feat_hbm.1, bf16[1024,2048]{1,0:T(8,128)(2,1)} %w_hbm.1, f32[64,2048]{1,0:T(8,128)S(1)} %copy-done, s32[2,2,128]{2,1,0:T(2,128)S(1)} %bitcast.1), custom_call_target="tpu_custom_call" | custom-call | tf_op jit(solution)/shard_map/pallas_call | solution.py:567
  75.4 2.0 %copy.8 = bf16[1024,2048]{1,0:T(8,128)(2,1)} copy(bf16[1024,2048]{1,0:T(8,128)(2,1)S(1)} %get-tuple-element.4) | data formatting | bytes 8388608
  77.4 0.8 %copy.9 = f32[128,1024]{1,0:T(8,128)} copy(f32[128,1024]{1,0:T(8,128)S(1)} %get-tuple-element.5) | data formatting | bytes 1048576
Async XLA Ops:
  0.6 1.0 %copy-start = (f32[64,2048]{1,0:T(8,128)S(1)}, f32[64,2048]{1,0:T(8,128)}, u32[]{:S(2)}) copy-start(f32[64,2048]{1,0:T(8,128)} %u_hbm.1) | copy-start | bytes 1572868
  1.7 0.7 copy-start.1

commit v4 on v3

--- a/solution.py
+++ b/solution.py
@@ -229,11 +229,13 @@
         pending = []
         sends = [0]
         partner = at_mp(z, h, 1 - core)
+        right, left, onward = at_dp(x + 1, l), at_dp(x - 1, l), at_dp(x + way, l)
 
         def send(src, dst, landed, device, when=None):
             sent = sends[0]
             sends[0] += 1
-            make = lambda: remote(src, dst, sent, landed, device)
+            made = lambda ref: ref() if callable(ref) else ref
+            make = lambda: remote(made(src), made(dst), sent, landed, device)
             if when is None:
                 make().start()
             else:
@@ -243,15 +245,15 @@
         def send_sum(slot, half):
             round_sum(slot, half)
             if half == 0:
-                send(sums.at[slot, 0], from_left.at[slot - 1], left_landed + slot - 1, at_dp(x + 1, l))
+                send(lambda: sums.at[slot, 0], lambda: from_left.at[slot - 1], left_landed + slot - 1, right)
             else:
-                send(sums.at[slot, 1], from_right.at[slot - 1], right_landed + slot - 1, at_dp(x - 1, l))
+                send(lambda: sums.at[slot, 1], lambda: from_right.at[slot - 1], right_landed + slot - 1, left)
 
         def reduce_pairs(i):
             if i == 3:
                 round_sum(0, 0)
                 round_sum(0, 1)
-                send(sums.at[0], relay, relay_landed, at_dp(x + way, l))
+                send(lambda: sums.at[0], relay, relay_landed, onward)
             if i == 7:
                 send_sum(1, 1 - core)
             if i == 9:
@@ -301,12 +303,12 @@
                     send(part, target, part_landed + core, device, when=is_owner)
 
         if core == 0:
-            late = jnp.where((z == 1) | (z == 3), LAG, 0)
+            uneven = (z == 1) | (z == 3)
+            follower = jnp.logical_not(is_source)
             early_set = jnp.where(z == 3, 1, 0)
-            send_base = 0
 
             def piece(i, half):
-                return win.at[lax.div(i, 4), lax.rem(i, 4), half]
+                return win.at[i // 4, i % 4, half]
 
             def routes(half):
                 step = 1 - 2 * half
@@ -356,17 +358,22 @@
                 arrived(piece(i, half), piece_landed + 2 * i + half)
                 pass_on(i, half)
 
-            for step in range(STEPS + LAG):
-                if step < STEPS:
-                    pl.when(jnp.logical_not(is_source))(lambda: take_piece(step, early_set))
-                index = step - late
-                ready = jnp.logical_not(is_source) & (index >= 0) & (index < STEPS)
-                pl.when(ready)(lambda: take_piece(index, 1 - early_set))
-                i = step - LAG
-                if i >= 0:
-                    product(i)
-                    reduce_pairs(i)
-
+            def relay_all(trail, lag):
+                for step in range(STEPS + lag):
+                    if step < STEPS:
+                        pl.when(follower)(lambda: take_piece(step, early_set))
+                    if 0 <= step - trail < STEPS:
+                        pl.when(follower)(lambda: take_piece(step - trail, 1 - early_set))
+                    i = step - lag
+                    if i >= 0:
+                        product(i)
+                        reduce_pairs(i)
+
+            mark = (sends[0], len(pending))
+            pl.when(uneven)(lambda: relay_all(LAG, LAG))
+            sends[0] = mark[0]
+            del pending[mark[1] :]
+            pl.when(jnp.logical_not(uneven))(lambda: relay_all(0, 1))
             send_pair()
             arrived(inv, inverse_landed)
             arrived(wcb.at[:, :, 0], rows_landed)
@@ -379,7 +386,7 @@
             finish_hessian()
             for i in range(STEPS):
                 for half in range(2):
-                    for when, copy in copies(jnp.int32(i), half):
+                    for when, copy in copies(i, half):
                         if when is None:
                             copy.wait_send()
                         else:
@@ -509,28 +516,27 @@
             send_weights()
             start_c()
             transpose_features()
+            u_gather.second()
             c_gather.second()
+            start_w()
+            w_gather.second()
+            third_u()
             c_gather.third()
-            u_gather.second()
-            start_w()
+            consume(0)
+            consume(1)
+            w_gather.third()
+            consume(2)
+            consume(3)
             c_gather.finish()
-            consume(0)
             invert_diagonal()
-            invert_level(0)
-            invert_level(1)
-            w_gather.second()
-            consume(1)
-            invert_level(2)
-            invert_level(3)
-            consume(2)
-            third_u()
-            consume(3)
-            for n in range(4, 7):
+            for n in range(3):
                 invert_level(n)
-            w_gather.third()
             consume(4)
+            for n in range(3, 6):
+                invert_level(n)
+            consume(5)
+            invert_level(6)
             invert_halves()
-            consume(5)
             invert_whole()
             finish_u()
             consume(6)

time: 78.3 us -> 75.2 us (0.960)
  the two profiles are of different devices: /device:TPU:24 before, /device:TPU:35 now
where the time goes in v4:
time: 75.2 us; the launch traced here: 75.1 us
  Pallas kernels  69.9 us (93%)
  local copies, waits for them, and re-layouts  4.52 us (6%)
    pallas_call x1, Pallas kernels, body(): pl.pallas_call(kernel, out_shape=(jax.ShapeDtypeStruct((1024, LOCAL_COLS)...  69.9 us
    unnamed x6, local copies, waits for them, and re-layouts  4.52 us

profile of v4, /device:TPU:35, one launch (start us, length us, event | category | flops | bytes accessed | tf_op | source)
XLA Modules:
  0.0 75.1 jit_solution(2326943741720140458)
XLA Ops:
  0.6 0.0 copy-start
  0.6 1.0 %copy-done = f32[64,2048]{1,0:T(8,128)S(1)} copy-done((f32[64,2048]{1,0:T(8,128)S(1)}, f32[64,2048]{1,0:T(8,128)}, u32[]{:S(2)}) %copy-start) | copy-done | bytes 524312
  1.7 0.0 copy-start.1
  1.7 0.7 copy-done.1
  2.4 69.9 %shard_map.59 = (bf16[1024,2048]{1,0:T(8,128)(2,1)S(1)}, f32[128,1024]{1,0:T(8,128)S(1)}) custom-call(bf16[2048,1024]{1,0:T(8,128)(2,1)} %feat_hbm.1, bf16[1024,2048]{1,0:T(8,128)(2,1)} %w_hbm.1, f32[64,2048]{1,0:T(8,128)S(1)} %copy-done, s32[2,2,128]{2,1,0:T(2,128)S(1)} %bitcast.1), custom_call_target="tpu_custom_call" | custom-call | tf_op jit(solution)/shard_map/pallas_call | solution.py:573
  72.2 2.0 %copy.8 = bf16[1024,2048]{1,0:T(8,128)(2,1)} copy(bf16[1024,2048]{1,0:T(8,128)(2,1)S(1)} %get-tuple-element.4) | data formatting | bytes 8388608
  74.3 0.8 %copy.9 = f32[128,1024]{1,0:T(8,128)} copy(f32[128,1024]{1,0:T(8,128)S(1)} %get-tuple-element.5) | data formatting | bytes 1048576
Async XLA Ops:
  0.6 1.0 %copy-start = (f32[64,2048]{1,0:T(8,128)S(1)}, f32[64,2048]{1,0:T(8,128)}, u32[]{:S(2)}) copy-start(f32[64,2048]{1,0:T(8,128)} %u_hbm.1) | copy-start | bytes 1572868
  1.7 0.7 copy-start.1

commit v5 on v4

--- a/solution.py
+++ b/solution.py
@@ -522,19 +522,17 @@
             w_gather.second()
             third_u()
             c_gather.third()
-            consume(0)
-            consume(1)
+            for i in range(4):
+                consume(i)
             w_gather.third()
-            consume(2)
-            consume(3)
+            consume(4)
             c_gather.finish()
             invert_diagonal()
             for n in range(3):
                 invert_level(n)
-            consume(4)
+            consume(5)
             for n in range(3, 6):
                 invert_level(n)
-            consume(5)
             invert_level(6)
             invert_halves()
             invert_whole()

time: 75.2 us -> 71.1 us (0.945)
  the two profiles are of different devices: /device:TPU:35 before, /device:TPU:59 now
where the time goes in v5:
time: 71.1 us; the launch traced here: 70.1 us
  Pallas kernels  65 us (91%)
  local copies, waits for them, and re-layouts  4.52 us (6%)
    pallas_call x1, Pallas kernels, body(): pl.pallas_call(kernel, out_shape=(jax.ShapeDtypeStruct((1024, LOCAL_COLS)...  65 us
    unnamed x6, local copies, waits for them, and re-layouts  4.52 us

profile of v5, /device:TPU:59, one launch (start us, length us, event | category | flops | bytes accessed | tf_op | source)
XLA Modules:
  0.0 70.1 jit_solution(13409711340204950628)
XLA Ops:
  0.6 0.0 copy-start
  0.6 1.0 %copy-done = f32[64,2048]{1,0:T(8,128)S(1)} copy-done((f32[64,2048]{1,0:T(8,128)S(1)}, f32[64,2048]{1,0:T(8,128)}, u32[]{:S(2)}) %copy-start) | copy-done | bytes 524312
  1.7 0.0 copy-start.1
  1.7 0.7 copy-done.1
  2.4 65.0 %shard_map.59 = (bf16[1024,2048]{1,0:T(8,128)(2,1)S(1)}, f32[128,1024]{1,0:T(8,128)S(1)}) custom-call(bf16[2048,1024]{1,0:T(8,128)(2,1)} %feat_hbm.1, bf16[1024,2048]{1,0:T(8,128)(2,1)} %w_hbm.1, f32[64,2048]{1,0:T(8,128)S(1)} %copy-done, s32[2,2,128]{2,1,0:T(2,128)S(1)} %bitcast.1), custom_call_target="tpu_custom_call" | custom-call | tf_op jit(solution)/shard_map/pallas_call | solution.py:571
  67.3 2.0 %copy.8 = bf16[1024,2048]{1,0:T(8,128)(2,1)} copy(bf16[1024,2048]{1,0:T(8,128)(2,1)S(1)} %get-tuple-element.4) | data formatting | bytes 8388608
  69.3 0.8 %copy.9 = f32[128,1024]{1,0:T(8,128)} copy(f32[128,1024]{1,0:T(8,128)S(1)} %get-tuple-element.5) | data formatting | bytes 1048576
Async XLA Ops:
  0.6 1.0 %copy-start = (f32[64,2048]{1,0:T(8,128)S(1)}, f32[64,2048]{1,0:T(8,128)}, u32[]{:S(2)}) copy-start(f32[64,2048]{1,0:T(8,128)} %u_hbm.1) | copy-start | bytes 1572868
  1.7 0.7 copy-start.1
